TPU v7x, 32 devices: a whole 2x2x4 slice. The times are simulated.
32 devices in a mesh: row: 4 (over x, core), col: 2 (over y), layer: 4 (over z).
Axes of the slice: x: 2, y: 2, z: 4, core: 2. Of those that a mesh axis runs over, the one named last changes fastest.
Arguments:
- density_matrix: bfloat16 [2048, 2048], P('row', 'col'), may hold values from -3 to 3
- block_mask: int32 [32, 32], P('row', 'col'), may hold values 0 or 1
- intersection_weights: float32 [2048], P(('col', 'layer')), may hold values from -0.125 to 0.125
- exponents: float32 [2048], P('row'), may hold values from 0.5 to 8
- anchor_x: int32 [32], P('row'), may hold values from 0 to 31
- anchor_y: int32 [32], P('row'), may hold values from 0 to 127, as said below
- anchor_z: int32 [32], P('row'), may hold values from 0 to 127
Outputs:
- squared: bfloat16 [2048, 2048], P('row', ('col', 'layer'))
- density: float32 [128, 128, 128], P('row', ('col', 'layer'))
Inputs may be any that keep to these rules, and one draw needn't show every extreme that they name: `anchor_y`: block row a starts in the second dimension between (a mod (8)) * 16 and that plus 16 - 1.
All inputs are finite; a program needn't handle non-finite values. No bound on the sum of `block_mask` on one device may be relied on, other than what follows from the above.
Results may differ from a plain program's by a relative error of at most 0.0055.
Values may be sent and summed in bfloat16 or wider, within the bound.
A program may use at most 64 MiB of HBM per device.

v0:
```python
import jax
import jax.numpy as jnp
from jax import lax
from jax.sharding import PartitionSpec as P

BLOCK = 64
TILE = 16
SX = 32
SY = 16
GZ = 128


grid_step_sq = 0.0625


def broadcast(block, axis, source):
    block = jnp.where(lax.axis_index(axis) == source, block, jnp.zeros_like(block))
    return lax.psum(block, axis)


def shifted(block, axis, distance):
    devices = range(lax.axis_size(axis))
    route = [((i - distance) % len(devices), i) for i in devices]
    return lax.ppermute(block, axis, route)


def local(
    density_matrix, block_mask, intersection_weights, exponents, anchor_x, anchor_y, anchor_z
):
    row_count = lax.axis_size("row")
    col_count = lax.axis_size("col")
    layer_count = lax.axis_size("layer")
    rows_here = density_matrix.shape[0]
    cols_here = density_matrix.shape[1]
    col_ratio = row_count // col_count
    layer_at = lax.axis_index("layer")
    wide_mask = jnp.repeat(jnp.repeat(block_mask, BLOCK, 0), BLOCK, 1)
    masked = jnp.where(wide_mask > 0, density_matrix, jnp.zeros_like(density_matrix))
    width = cols_here // layer_count
    own_cols = lax.dynamic_slice_in_dim(masked, layer_at * width, width, 1)
    running = jnp.zeros((rows_here, width), jnp.float32)
    for inner_at in range(row_count):
        left_part = lax.dynamic_slice_in_dim(masked, inner_at % col_ratio * rows_here, rows_here, 1)
        left_part = broadcast(left_part, "col", inner_at // col_ratio)
        right_part = broadcast(own_cols, "row", inner_at)
        running = running + jnp.dot(left_part, right_part, preferred_element_type=jnp.float32)
    squared = running.astype(jnp.bfloat16)
    partial_charges = jnp.dot(running, intersection_weights, precision=lax.Precision.HIGHEST)
    charges = lax.psum(partial_charges, ("col", "layer"))
    atom_count = anchor_x.shape[0]
    y_index = lax.axis_index("col") * layer_count + layer_at
    offsets = jnp.arange(TILE, dtype=jnp.int32)
    centre = offsets.astype(jnp.float32) - 7.5
    atom_charges = charges.reshape(atom_count, BLOCK)
    decay_rates = exponents.reshape(atom_count, BLOCK)
    profiles = jnp.exp(-decay_rates[:, :, None] * grid_step_sq * centre[None, None, :] ** 2)
    all_tiles = jnp.einsum(
        "ak,akx,aky,akz->axyz",
        atom_charges,
        profiles,
        profiles,
        profiles,
        precision=lax.Precision.HIGHEST,
    )

    def deposit(atom_at, buffer):
        start_y = anchor_y[atom_at] - y_index * SY
        is_owned = (start_y >= 0) & (start_y < SY)
        start_y = jnp.where(is_owned, start_y, 0)
        weight = jnp.where(is_owned, 1.0, 0.0).astype(jnp.float32)
        tile_values = lax.dynamic_index_in_dim(all_tiles, atom_at, 0, keepdims=False)
        start_x = anchor_x[atom_at]
        start_z = anchor_z[atom_at]
        current = lax.dynamic_slice(buffer, (start_x, start_y, start_z), (TILE, TILE, TILE))
        return lax.dynamic_update_slice(
            buffer, current + weight * tile_values, (start_x, start_y, start_z)
        )

    buffer = lax.fori_loop(
        0, atom_count, deposit, jnp.zeros((SX + TILE, SY + TILE, GZ + TILE), jnp.float32)
    )
    buffer = buffer[:, :, :GZ].at[:, :, :TILE].add(buffer[:, :, GZ:])
    rim_x = buffer[SX:]
    came_x = shifted(rim_x.astype(jnp.bfloat16), "row", 1).astype(rim_x.dtype)
    base = buffer[:SX].at[:TILE].add(came_x)
    rim_y = base[:, SY:]
    came_y = shifted(rim_y.astype(jnp.bfloat16), ("col", "layer"), 1).astype(rim_y.dtype)
    density = base[:, :SY].at[:, :TILE].add(came_y)
    return (squared, density)


def solution(mesh):
    return jax.shard_map(
        local,
        mesh=mesh,
        in_specs=(
            P("row", "col"),
            P("row", "col"),
            P(("col", "layer")),
            P("row"),
            P("row"),
            P("row"),
            P("row"),
        ),
        out_specs=(P("row", ("col", "layer")), P("row", ("col", "layer"), None)),
        check_vma=False,
    )
```

profile of v0, /device:TPU:0, one launch (start us, length us, event | category | flops | bytes accessed | tf_op | source)
XLA Modules:
  0.0 261.5 jit_solution(14411166556518656421)
XLA Ops:
  7.2 1.5 copy.11
  9.2 1.1 broadcast_select_fusion.4
  10.3 1.4 broadcast_select_fusion
  11.7 0.6 copy-done.7
  12.5 37.8 %all-reduce.5.cloned.1.call-done = (bf16[512,256]{0,1:T(8,128)(2,1)}, bf16[512,256]{0,1:T(8,128)(2,1)}, bf16[512,256]{0,1:T(8,128)(2,1)}, bf16[512,256]{0,1:T(8,128)(2,1)}) async-done(((bf16[512,256]{0,1:T(8,128)(2,1)}, bf16[512,256]{0,1:T(8,128)(2,1)}, bf16[512,256]{0,1:T(8,128)(2,1)}, bf16[512,256]{0,1:T(8,128)(2,1)}), (bf16[512,256]{0,1:T(8,128)(2,1)}, bf16[512,256]{0,1:T(8,128)(2,1)}, ...) | async-done | bytes 1048592 | tf_op jit(solution)/shard_map/psum | solution.py:18
  50.3 66.0 %all-reduce.7.cloned.1.call-done = (bf16[512,512]{0,1:T(8,128)(2,1)}, bf16[512,512]{0,1:T(8,128)(2,1)}, bf16[512,512]{0,1:T(8,128)(2,1)}, bf16[512,512]{0,1:T(8,128)(2,1)}) async-done(((bf16[512,512]{0,1:T(8,128)(2,1)}, bf16[512,512]{0,1:T(8,128)(2,1)}, bf16[512,512]{0,1:T(8,128)(2,1)}, bf16[512,512]{0,1:T(8,128)(2,1)}), (bf16[512,512]{0,1:T(8,128)(2,1)}, bf16[512,512]{0,1:T(8,128)(2,1)}, ...) | async-done | bytes 2097168 | tf_op jit(solution)/shard_map/psum | solution.py:18
  116.3 1.6 fusion.8
  117.9 1.4 convolution_add_fusion.2
  119.7 1.0 fusion.7
  121.4 20.6 %psum.71 = f32[8,64]{1,0:T(8,128)S(1)} all-reduce(f32[8,64]{1,0:T(8,128)S(1)} %reshape.127), channel_id=1, replica_groups=mesh['row'=4,'col'=2,'layer'=4] {'col','layer'}, use_global_device_ids=true, to_apply=%region_8.9 | all-reduce | flops 512 | bytes 4096 | tf_op jit(solution)/shard_map/psum | solution.py:49
  141.9 1.1 convolution_bitcast_fusion
  143.2 96.2 %while.19 = (s32[]{:T(128)}, f32[48,32,144]{2,1,0:T(8,128)S(1)}, s32[8]{0:T(128)S(1)}, s32[8]{0:T(128)S(1)}, s32[]{:T(128)}, /*index=5*/s32[8]{0:T(128)S(1)}, f3...) while((s32[]{:T(128)}, f32[48,32,144]{2,1,0:T(8,128)S(1)}, ...), condition=%wide.region_10.11_spmd, body=%wide.region_9.10_spmd.sunk | while | flops 8209 | bytes 147826 | solution.py:79
  143.4 0.6 dynamic_slice.79
  145.9 0.6 dynamic_slice.80
  147.2 0.6 dynamic_slice.81
  149.8 5.4 %dynamic_update_slice.10 = f32[48,32,144]{2,1,0:T(8,128)S(1)} dynamic-update-slice(f32[48,32,144]{2,1,0:T(8,128)S(1)} %get-tuple-element.322, f32[16,16,16]{2,1,0:T(8,128)S(1)} %bitcast_add_fusion.2, s32[]{:T(128)S(6)} %select_n.154, s32[]{:T(128)S(6)} %select_n.156, s32[]{:T(128)S(6)} %select_n.157) | dynamic-update-slice | bytes 32772 | tf_op jit(solution)/shard_map/while/body/eval_jaxpr/dynamic_update_slice | solution.py:75
  155.4 0.6 dynamic_slice.79
  157.9 0.6 dynamic_slice.80
  159.2 0.6 dynamic_slice.81
  161.8 5.4 %dynamic_update_slice.10 = f32[48,32,144]{2,1,0:T(8,128)S(1)} dynamic-update-slice(f32[48,32,144]{2,1,0:T(8,128)S(1)} %get-tuple-element.322, f32[16,16,16]{2,1,0:T(8,128)S(1)} %bitcast_add_fusion.2, s32[]{:T(128)S(6)} %select_n.154, s32[]{:T(128)S(6)} %select_n.156, s32[]{:T(128)S(6)} %select_n.157) | dynamic-update-slice | bytes 32772 | tf_op jit(solution)/shard_map/while/body/eval_jaxpr/dynamic_update_slice | solution.py:75
  167.4 0.6 dynamic_slice.79
  169.9 0.6 dynamic_slice.80
  171.2 0.6 dynamic_slice.81
  173.9 5.4 %dynamic_update_slice.10 = f32[48,32,144]{2,1,0:T(8,128)S(1)} dynamic-update-slice(f32[48,32,144]{2,1,0:T(8,128)S(1)} %get-tuple-element.322, f32[16,16,16]{2,1,0:T(8,128)S(1)} %bitcast_add_fusion.2, s32[]{:T(128)S(6)} %select_n.154, s32[]{:T(128)S(6)} %select_n.156, s32[]{:T(128)S(6)} %select_n.157) | dynamic-update-slice | bytes 32772 | tf_op jit(solution)/shard_map/while/body/eval_jaxpr/dynamic_update_slice | solution.py:75
  179.4 0.6 dynamic_slice.79
  182.0 0.6 dynamic_slice.80
  183.2 0.6 dynamic_slice.81
  185.9 5.4 %dynamic_update_slice.10 = f32[48,32,144]{2,1,0:T(8,128)S(1)} dynamic-update-slice(f32[48,32,144]{2,1,0:T(8,128)S(1)} %get-tuple-element.322, f32[16,16,16]{2,1,0:T(8,128)S(1)} %bitcast_add_fusion.2, s32[]{:T(128)S(6)} %select_n.154, s32[]{:T(128)S(6)} %select_n.156, s32[]{:T(128)S(6)} %select_n.157) | dynamic-update-slice | bytes 32772 | tf_op jit(solution)/shard_map/while/body/eval_jaxpr/dynamic_update_slice | solution.py:75
  191.5 0.6 dynamic_slice.79
  194.0 0.6 dynamic_slice.80
  195.2 0.6 dynamic_slice.81
  197.9 5.4 %dynamic_update_slice.10 = f32[48,32,144]{2,1,0:T(8,128)S(1)} dynamic-update-slice(f32[48,32,144]{2,1,0:T(8,128)S(1)} %get-tuple-element.322, f32[16,16,16]{2,1,0:T(8,128)S(1)} %bitcast_add_fusion.2, s32[]{:T(128)S(6)} %select_n.154, s32[]{:T(128)S(6)} %select_n.156, s32[]{:T(128)S(6)} %select_n.157) | dynamic-update-slice | bytes 32772 | tf_op jit(solution)/shard_map/while/body/eval_jaxpr/dynamic_update_slice | solution.py:75
  203.5 0.6 dynamic_slice.79
  206.0 0.6 dynamic_slice.80
  207.3 0.6 dynamic_slice.81
  209.9 5.4 %dynamic_update_slice.10 = f32[48,32,144]{2,1,0:T(8,128)S(1)} dynamic-update-slice(f32[48,32,144]{2,1,0:T(8,128)S(1)} %get-tuple-element.322, f32[16,16,16]{2,1,0:T(8,128)S(1)} %bitcast_add_fusion.2, s32[]{:T(128)S(6)} %select_n.154, s32[]{:T(128)S(6)} %select_n.156, s32[]{:T(128)S(6)} %select_n.157) | dynamic-update-slice | bytes 32772 | tf_op jit(solution)/shard_map/while/body/eval_jaxpr/dynamic_update_slice | solution.py:75
  215.5 0.6 dynamic_slice.79
  218.0 0.6 dynamic_slice.80
  219.3 0.6 dynamic_slice.81
  221.9 5.4 %dynamic_update_slice.10 = f32[48,32,144]{2,1,0:T(8,128)S(1)} dynamic-update-slice(f32[48,32,144]{2,1,0:T(8,128)S(1)} %get-tuple-element.322, f32[16,16,16]{2,1,0:T(8,128)S(1)} %bitcast_add_fusion.2, s32[]{:T(128)S(6)} %select_n.154, s32[]{:T(128)S(6)} %select_n.156, s32[]{:T(128)S(6)} %select_n.157) | dynamic-update-slice | bytes 32772 | tf_op jit(solution)/shard_map/while/body/eval_jaxpr/dynamic_update_slice | solution.py:75
  227.5 0.6 dynamic_slice.79
  230.1 0.6 dynamic_slice.80
  231.3 0.6 dynamic_slice.81
  234.0 5.4 %dynamic_update_slice.10 = f32[48,32,144]{2,1,0:T(8,128)S(1)} dynamic-update-slice(f32[48,32,144]{2,1,0:T(8,128)S(1)} %get-tuple-element.322, f32[16,16,16]{2,1,0:T(8,128)S(1)} %bitcast_add_fusion.2, s32[]{:T(128)S(6)} %select_n.154, s32[]{:T(128)S(6)} %select_n.156, s32[]{:T(128)S(6)} %select_n.157) | dynamic-update-slice | bytes 32772 | tf_op jit(solution)/shard_map/while/body/eval_jaxpr/dynamic_update_slice | solution.py:75
  239.6 2.0 scatter-add.6
  241.8 4.3 %collective-permute-done = bf16[16,32,128]{2,1,0:T(8,128)(2,1)S(1)} collective-permute-done((bf16[16,32,128]{2,1,0:T(8,128)(2,1)S(1)}, bf16[16,32,128]{2,1,0:T(8,128)(2,1)S(1)}, u32[]{:S(2)}, u32[]{:S(2)}) %collective-permute-start) | collective-permute-done | bytes 131104 | tf_op jit(solution)/shard_map/ppermute | solution.py:24
  246.2 7.7 %collective-permute-done.1 = bf16[32,16,128]{2,1,0:T(8,128)(2,1)S(1)} collective-permute-done((bf16[32,16,128]{2,1,0:T(8,128)(2,1)S(1)}, bf16[32,16,128]{2,1,0:T(8,128)(2,1)S(1)}, u32[]{:S(2)}, u32[]{:S(2)}) %collective-permute-start.1) | collective-permute-done | bytes 131104 | tf_op jit(solution)/shard_map/ppermute | solution.py:24
  253.9 0.7 slice_add_fusion.1
  (70 shorter events, 4.3 us)
Async XLA Ops:
  7.2 113.6 %copy-start = (f32[256]{0:T(256)S(1)}, f32[256]{0:T(256)}, u32[]{:S(2)}) copy-start(f32[256]{0:T(256)} %param.19) | copy-start | bytes 3076
  7.2 1.6 copy-start.6
  7.2 43.1 %all-reduce.5.cloned.1.call-start = ((), (), s32[]{:S(2)}) async-start(), calls=%async_computation | async-start | bytes 2097152 | tf_op jit(solution)/shard_map/psum | solution.py:18
  10.2 106.1 %all-reduce.7.cloned.1.call-start = ((), (), s32[]{:S(2)}) async-start(), calls=%async_computation.1 | async-start | bytes 4194304 | tf_op jit(solution)/shard_map/psum | solution.py:18
  11.7 0.7 copy-start.7
  116.3 1.6 copy-start.2
  116.3 3.0 %copy-start.1 = (bf16[512,512]{0,1:T(8,128)(2,1)S(1)}, bf16[512,512]{0,1:T(8,128)(2,1)}, u32[]{:S(2)}) copy-start(bf16[512,512]{0,1:T(8,128)(2,1)} %get-tuple-element.251) | copy-start | bytes 1572868
  116.3 3.0 %copy-start.4 = (bf16[512,256]{0,1:T(8,128)(2,1)S(1)}, bf16[512,256]{0,1:T(8,128)(2,1)}, u32[]{:S(2)}) copy-start(bf16[512,256]{0,1:T(8,128)(2,1)} %get-tuple-element.247) | copy-start | bytes 786436
  117.9 1.8 copy-start.3
  117.9 1.8 copy-start.5
  120.7 22.4 %copy-start.8 = (s32[8]{0:T(128)S(1)}, s32[8]{0:T(128)}, u32[]{:S(2)}) copy-start(s32[8]{0:T(128)} %param.21) | copy-start | bytes 100
  120.7 22.4 %copy-start.9 = (s32[8]{0:T(128)S(1)}, s32[8]{0:T(128)}, u32[]{:S(2)}) copy-start(s32[8]{0:T(128)} %param.22) | copy-start | bytes 100
  120.7 22.5 %copy-start.10 = (s32[8]{0:T(128)S(1)}, s32[8]{0:T(128)}, u32[]{:S(2)}) copy-start(s32[8]{0:T(128)} %param.23) | copy-start | bytes 100
  241.7 4.4 %collective-permute-start = (bf16[16,32,128]{2,1,0:T(8,128)(2,1)S(1)}, bf16[16,32,128]{2,1,0:T(8,128)(2,1)S(1)}, u32[]{:S(2)}, u32[]{:S(2)}) collective-permute-start(bf16[16,32,128]{2,1,0:T(8,128)(2,1)S(1)} %slice.111), channel_id=1, source_target_pairs={{24,0},{0,8},{8,16},{16,24},{25,1},{1,9},{9,17},{17,25},{26,2},{2,... | collective-permute-start | bytes 393224 | tf_op jit(solution)/shard_map/ppermute | solution.py:24
  246.2 7.7 %collective-permute-start.1 = (bf16[32,16,128]{2,1,0:T(8,128)(2,1)S(1)}, bf16[32,16,128]{2,1,0:T(8,128)(2,1)S(1)}, u32[]{:S(2)}, u32[]{:S(2)}) collective-permute-start(bf16[32,16,128]{2,1,0:T(8,128)(2,1)S(1)} %slice.110), channel_id=1, source_target_pairs={{7,0},{0,1},{1,2},{2,3},{3,4},{4,5},{5,6},{6,7},{15,8},{8,9},{9,10... | collective-permute-start | bytes 393224 | tf_op jit(solution)/shard_map/ppermute | solution.py:24
Sparse Core Ops, SparseCore 0:
  11.1 39.1 all-reduce.4
  52.8 63.5 all-reduce.6
where the time goes:
time: 262 us; the launch traced here: 261 us
  waiting for transfers between devices  116 us (44%)
  local copies, waits for them, and re-layouts  63.4 us (24%)
  loops' own time  36.8 us (14%)
  blocking collectives  20.6 us (8%)
  between operations  14.3 us (5%)
  matrix products  5.91 us (2%)
  other arithmetic  4.43 us (2%)
    psum x2, waiting for transfers between devices, broadcast(): return lax.psum(block, axis)  104 us
    dynamic_update_slice x8, local copies, waits for them, and re-layouts, deposit(): lax.dynamic_update_slice(buffer, current + weight * tile_values, (start_x...  43.1 us
    another operation x1, loops' own time, local(): lax.fori_loop(0, atom_count, deposit, jnp.zeros((SX + TILE, SY + TILE, GZ...  36.8 us
    psum x1, blocking collectives, local(): charges = lax.psum(partial_charges, ('col', 'layer'))  20.6 us
    ppermute x2, waiting for transfers between devices, shifted(): return lax.ppermute(block, axis, route)  12 us
  transfers between devices with their start and end apart: 4, of which 4 were waited for; matrix products, arithmetic and copies ran while one was open for 1% of the time, Pallas kernels for 0%

commit v1 on v0

v1 whole, which is shorter than its diff:
```python
import functools

import jax
import jax.numpy as jnp
from jax import lax
from jax.experimental import pallas as pl
from jax.experimental.pallas import tpu as pltpu
from jax.sharding import PartitionSpec as P

BLOCK = 64
TILE = 16
SX = 32
SY = 16
GZ = 128
STEP_SQ = 0.0625
MESH = pl.DeviceIdType.MESH
F32 = jnp.float32
BF16 = jnp.bfloat16
IN_CHUNKS = 2
OUT_CHUNKS = 4


def dot_nt(a, b):
    return lax.dot_general(a, b, (((1,), (1,)), ((), ())), preferred_element_type=F32)


def hi_lo(x):
    high = x.astype(BF16).astype(F32)
    return jnp.concatenate([high, x - high], axis=0).astype(BF16)


def kernel(
    sizes,
    a_ref, mask_ref, w_ref, e_ref, ax_ref, ay_ref, az_ref,
    sq_ref, den_ref,
    m_buf, right, part_out, part_in, w_all, v_out, v_all, q_out, q_all, pack, pack_in, shape_xy, shape_z,
    piece_send, piece_recv, fwd_send, part_send, part_recv,
    w_send, w_recv, v_send, v_recv, q_send, q_recv, pack_send, pack_recv,
):
    nr, nc, nl = sizes
    ratio = nr // nc
    rows, cols = a_ref.shape
    width = cols // nl
    atoms = rows // BLOCK
    r, c, l = lax.axis_index("row"), lax.axis_index("col"), lax.axis_index("layer")
    sibling = r + 1 - 2 * (r % 2)
    following = (r + 1) % nr

    def remote(src, dst, send, recv, device):
        return pltpu.make_async_remote_copy(
            src_ref=src, dst_ref=dst, send_sem=send, recv_sem=recv,
            device_id=device, device_id_type=MESH,
        )

    barrier = pltpu.get_barrier_semaphore()
    peers = 0
    for dr in range(nr):
        for dc in range(nc):
            if dr or dc:
                peers += 1
                pl.semaphore_signal(
                    barrier, inc=1, device_id=((r + dr) % nr, (c + dc) % nc, l), device_id_type=MESH
                )
    for k in range(1, nl):
        peers += 1
        pl.semaphore_signal(barrier, inc=1, device_id=(r, c, (l + k) % nl), device_id_type=MESH)

    kept = jnp.where(mask_ref[...] > 0, 1.0, 0.0).astype(F32)
    spread = lax.broadcasted_iota(jnp.int32, (cols // BLOCK, cols), 1) // BLOCK
    pick = lax.broadcasted_iota(jnp.int32, (cols // BLOCK, cols), 0)
    wide = jnp.dot(kept, jnp.where(spread == pick, 1.0, 0.0).astype(F32), preferred_element_type=F32)
    for b in range(atoms):
        at = pl.ds(b * BLOCK, BLOCK)
        m_buf[at, :] = a_ref[at, :] * jnp.broadcast_to(wide[b : b + 1, :], (BLOCK, cols)).astype(BF16)
    w_all[l] = jnp.broadcast_to(w_ref[...], (8, width))
    lane_atom = lax.broadcasted_iota(jnp.int32, (8, rows), 1) // BLOCK
    sub = lax.broadcasted_iota(jnp.int32, (8, rows), 0)
    table = jnp.broadcast_to(e_ref[...], (8, rows))
    for j in range(atoms):
        here = lane_atom == j
        for at, ref in ((1, ax_ref), (2, ay_ref), (3, az_ref)):
            table = jnp.where(here & (sub == at), ref[j].astype(F32), table)
    pack[...] = table

    pl.semaphore_wait(barrier, peers)

    w_copies = [
        remote(w_all.at[l], w_all.at[l], w_send.at[k - 1], w_recv.at[k - 1], (r, c, (l + k) % nl))
        for k in range(1, nl)
    ]
    for copy in w_copies:
        copy.start()
    pack_copy = remote(pack, pack_in, pack_send.at[0], pack_recv.at[0], (following, c, l))
    pack_copy.start()

    home = r // ratio
    slot = r % ratio
    step = rows // IN_CHUNKS

    def strip(h):
        return m_buf.at[pl.ds(h * step, step), pl.ds(pl.multiple_of(l * width, 128), width)]

    def piece(i, cc, h):
        return right.at[i, cc, pl.ds(h * step, step), :]

    def sem_at(i, cc, h):
        return (i * nc + cc) * IN_CHUNKS + h

    def piece_copy(k, h):
        return remote(
            strip(h), piece(slot, c, h), piece_send.at[k * IN_CHUNKS + h],
            piece_recv.at[sem_at(slot, c, h)], ((r + 2 * k) % nr, home, l),
        )

    def own_copy(h):
        return pltpu.make_async_copy(strip(h), piece(slot, c, h), piece_recv.at[sem_at(slot, c, h)])

    at_home = home == c
    for h in range(IN_CHUNKS):
        for k in range(1, nr // 2):
            piece_copy(k, h).start()

        @pl.when(at_home)
        def _():
            own_copy(h).start()

        @pl.when(jnp.logical_not(at_home))
        def _():
            piece_copy(0, h).start()

    for copy in w_copies:
        copy.wait_recv()
    total = jnp.zeros((16, rows), F32)
    for k in range(nl):
        total = total + dot_nt(hi_lo(w_all[k]), m_buf[:, k * width : (k + 1) * width])
    v_out[...] = total[:8] + total[8:]

    def v_copy(k):
        return remote(
            v_out, v_all.at[slot, c], v_send.at[k], v_recv.at[slot * nc + c], ((r + k) % nr, home, l)
        )

    @pl.when(at_home)
    def _():
        v_all[slot, c] = v_out[...]

    @pl.when(jnp.logical_not(at_home))
    def _():
        v_copy(0).start()

    for k in range(1, nr):
        v_copy(k).start()

    pack_copy.wait_recv()
    y_first = (c * nl + l) * SY
    y_count = nc * nl * SY
    for g, ref in ((0, pack), (1, pack_in)):
        rate = ref[0:1, :] * (-STEP_SQ)

        def profile(t):
            value = jnp.exp(rate * (t - 7.5) * (t - 7.5))
            return jnp.where((t >= 0.0) & (t < float(TILE)), value, 0.0)

        tx = lax.broadcasted_iota(jnp.int32, (SX, rows), 0).astype(F32) + float(g * SX) - ref[1:2, :]
        ty = (lax.broadcasted_iota(jnp.int32, (SY, rows), 0) + y_first).astype(F32) - ref[2:3, :]
        ty = jnp.where(ty < 0.0, ty + float(y_count), ty)
        tz = lax.broadcasted_iota(jnp.int32, (GZ, rows), 0).astype(F32) - ref[3:4, :]
        tz = jnp.where(tz < 0.0, tz + float(GZ), tz)
        px, py = profile(tx), profile(ty)
        for x in range(SX):
            shape_xy[g, x * SY : (x + 1) * SY, :] = (px[x : x + 1, :] * py).astype(BF16)
        shape_z[g] = profile(tz)

    def direct(i):
        return (c * ratio + i) % 2 == r % 2

    def fwd_copy(i, cc, h):
        return remote(
            piece(i, cc, h), piece(i, cc, h), fwd_send.at[sem_at(i, cc, h)],
            piece_recv.at[sem_at(i, cc, h)], (sibling, c, l),
        )

    def landed(i, cc, h):
        fwd_copy(i, cc, h).wait_recv()

    for h in range(IN_CHUNKS):
        for i in range(ratio):
            for k in range(nc):
                cc = (c + 1 + k) % nc

                @pl.when(direct(i))
                def _():
                    mine = (c * ratio + i == r) & (cc == c)

                    @pl.when(mine)
                    def _():
                        own_copy(h).wait()

                    @pl.when(jnp.logical_not(mine))
                    def _():
                        landed(i, cc, h)

                    fwd_copy(i, cc, h).start()

    for i in range(ratio):
        for cc in range(nc):

            @pl.when(jnp.logical_not((c * ratio + i == r) & (cc == c)))
            def _():
                remote(v_out, v_all.at[i, cc], v_send.at[0], v_recv.at[i * nc + cc], (r, c, l)).wait_recv()

    total = jnp.zeros((16, rows), F32)
    for i in range(ratio):
        v = v_all[i, 0]
        for cc in range(1, nc):
            v = v + v_all[i, cc]
        total = total + dot_nt(hi_lo(v), m_buf[:, i * rows : (i + 1) * rows])
    q_out[...] = total[:8] + total[8:]
    q_all[0, c] = q_out[...]

    def q_copy(g, k):
        return remote(
            q_out, q_all.at[g, c], q_send.at[g * nc + k], q_recv.at[g * nc + k],
            ((r + g) % nr, (c + k) % nc, l),
        )

    sent_q = [(g, k) for g in range(2) for k in range(nc) if g or k]
    for g, k in sent_q:
        q_copy(g, k).start()

    for h in range(IN_CHUNKS):
        for i in range(ratio):
            for k in range(nc):

                @pl.when(jnp.logical_not(direct(i)))
                def _():
                    landed(i, (c + 1 + k) % nc, h)

    tall = rows // OUT_CHUNKS

    def product(cc, o):
        at = pl.ds(o * tall, tall)
        total = jnp.dot(m_buf[at, 0:rows], right[0, cc], preferred_element_type=F32)
        for i in range(1, ratio):
            total = total + jnp.dot(
                m_buf[at, i * rows : (i + 1) * rows], right[i, cc], preferred_element_type=F32
            )
        return total

    def part_copy(k, o):
        at = pl.ds(o * tall, tall)
        index = (k - 1) * OUT_CHUNKS + o
        return remote(
            part_out.at[k - 1, at, :], part_in.at[k - 1, at, :], part_send.at[index],
            part_recv.at[index], (r, (c + k) % nc, l),
        )

    for k in range(1, nc):
        for o in range(OUT_CHUNKS):
            part_out[k - 1, o * tall : (o + 1) * tall, :] = product((c + k) % nc, o).astype(BF16)
            part_copy(k, o).start()

    for g, k in sent_q:
        q_copy(g, k).wait_recv()
    total = jnp.zeros((SX * SY, GZ), F32)
    for g in range(2):
        charge = q_all[g, 0]
        for cc in range(1, nc):
            charge = charge + q_all[g, cc]
        total = total + dot_nt(shape_xy[g], (shape_z[g] * charge[0:1, :]).astype(BF16))
    den_ref[...] = total.reshape(SX, SY, GZ)

    for o in range(OUT_CHUNKS):
        total = product(c, o)
        for k in range(1, nc):
            part_copy(k, o).wait_recv()
            total = total + part_in[k - 1, o * tall : (o + 1) * tall, :].astype(F32)
        sq_ref[o * tall : (o + 1) * tall, :] = total.astype(BF16)

    for copy in w_copies:
        copy.wait_send()
    pack_copy.wait_send()
    for k in range(1, nr):
        v_copy(k).wait_send()
    for g, k in sent_q:
        q_copy(g, k).wait_send()
    for h in range(IN_CHUNKS):
        for k in range(1, nr // 2):
            piece_copy(k, h).wait_send()
        for i in range(ratio):
            for cc in range(nc):

                @pl.when(direct(i))
                def _():
                    fwd_copy(i, cc, h).wait_send()

    @pl.when(jnp.logical_not(at_home))
    def _():
        v_copy(0).wait_send()
        for h in range(IN_CHUNKS):
            piece_copy(0, h).wait_send()

    for k in range(1, nc):
        for o in range(OUT_CHUNKS):
            part_copy(k, o).wait_send()


def local(sizes, density_matrix, block_mask, weights, exponents, anchor_x, anchor_y, anchor_z):
    nr, nc, nl = sizes
    ratio = nr // nc
    rows, cols = density_matrix.shape
    width = cols // nl
    dma = pltpu.SemaphoreType.DMA
    pieces = ratio * nc * IN_CHUNKS
    vmem = pl.BlockSpec(memory_space=pltpu.VMEM)
    smem = pl.BlockSpec(memory_space=pltpu.SMEM)
    return pl.pallas_call(
        functools.partial(kernel, sizes),
        out_shape=(
            jax.ShapeDtypeStruct((rows, width), BF16),
            jax.ShapeDtypeStruct((SX, SY, GZ), F32),
        ),
        in_specs=[vmem] * 4 + [smem] * 3,
        out_specs=(vmem, vmem),
        scratch_shapes=[
            pltpu.VMEM((rows, cols), BF16),
            pltpu.VMEM((ratio, nc, rows, width), BF16),
            pltpu.VMEM((nc - 1, rows, width), BF16),
            pltpu.VMEM((nc - 1, rows, width), BF16),
            pltpu.VMEM((nl, 8, width), F32),
            pltpu.VMEM((8, rows), F32),
            pltpu.VMEM((ratio, nc, 8, rows), F32),
            pltpu.VMEM((8, rows), F32),
            pltpu.VMEM((2, nc, 8, rows), F32),
            pltpu.VMEM((8, rows), F32),
            pltpu.VMEM((8, rows), F32),
            pltpu.VMEM((2, SX * SY, rows), BF16),
            pltpu.VMEM((2, GZ, rows), F32),
            dma((nr // 2 * IN_CHUNKS,)),
            dma((pieces,)),
            dma((pieces,)),
            dma(((nc - 1) * OUT_CHUNKS,)),
            dma(((nc - 1) * OUT_CHUNKS,)),
            dma((nl - 1,)),
            dma((nl - 1,)),
            dma((nr,)),
            dma((ratio * nc,)),
            dma((2 * nc,)),
            dma((2 * nc,)),
            dma((1,)),
            dma((1,)),
        ],
        compiler_params=pltpu.CompilerParams(
            collective_id=0, has_side_effects=True, vmem_limit_bytes=48 * 1024 * 1024
        ),
        name="square_collocate",
    )(
        density_matrix, block_mask, weights.reshape(1, -1), exponents.reshape(1, -1),
        anchor_x, anchor_y, anchor_z,
    )


def solution(mesh):
    sizes = (mesh.shape["row"], mesh.shape["col"], mesh.shape["layer"])
    return jax.shard_map(
        functools.partial(local, sizes),
        mesh=mesh,
        in_specs=(
            P("row", "col"), P("row", "col"), P(("col", "layer")),
            P("row"), P("row"), P("row"), P("row"),
        ),
        out_specs=(P("row", ("col", "layer")), P("row", ("col", "layer"), None)),
        check_vma=False,
    )
```

time: 262 us -> 29.9 us (0.11)
  waiting for transfers between devices: 116 us -> 0 us
  local copies, waits for them, and re-layouts: 63.4 us -> 5.3 us
  loops' own time: 36.8 us -> 0 us
  Pallas kernels: 0 us -> 23.7 us
  blocking collectives: 20.6 us -> 0 us
  between operations: 14.3 us -> 0.67 us
  matrix products: 5.91 us -> 0 us
  other arithmetic: 4.43 us -> 0 us
    psum x2 -> x0, waiting for transfers between devices: 104 us -> none  [broadcast(): return lax.psum(block, axis)]
    dynamic_update_slice x8 -> x0, local copies, waits for them, and re-layouts: 43.1 us -> none  [deposit(): lax.dynamic_update_slice(buffer, current + weight * tile_values, (start_x...]
    another operation x1 -> x0, loops' own time: 36.8 us -> none  [local(): lax.fori_loop(0, atom_count, deposit, jnp.zeros((SX + TILE, SY + TILE, GZ...]
    pallas_call x0 -> x1, Pallas kernels: none -> 23.7 us  [local(): pl.pallas_call(functools.partial(kernel, sizes), out_shape=(jax.ShapeDtyp...]
    psum x1 -> x0, blocking collectives: 20.6 us -> none  [local(): charges = lax.psum(partial_charges, ('col', 'layer'))]
    dynamic_slice x40 -> x0, local copies, waits for them, and re-layouts: 15.3 us -> none  [the longest x8 4.71 us: deposit(): start_z = anchor_z[atom_at]]
    ppermute x2 -> x0, waiting for transfers between devices: 12 us -> none  [shifted(): return lax.ppermute(block, axis, route)]
    dot_general x6 -> x0, matrix products: 5.91 us -> none  [the longest x4 4.32 us: local(): jnp.dot(left_part, right_part, preferred_element_type=jnp.float32)]
  transfers between devices with their start and end apart: 4 -> 0, of which waited for: 4 -> 0; matrix products, arithmetic and copies ran while one was open for 1% -> 0% of each run, Pallas kernels for 0% -> 0%
where the time goes in v1:
time: 29.9 us; the launch traced here: 29.7 us
  Pallas kernels  23.7 us (79%)
  local copies, waits for them, and re-layouts  5.3 us (18%)
  between operations  0.67 us (2%)
    pallas_call x1, Pallas kernels, local(): pl.pallas_call(functools.partial(kernel, sizes), out_shape=(jax.ShapeDtyp...  23.7 us
    unnamed x16, local copies, waits for them, and re-layouts  5.3 us

profile of v1, /device:TPU:0, one launch (start us, length us, event | category | flops | bytes accessed | tf_op | source)
XLA Modules:
  0.0 29.7 jit_solution(146490081513555550)
XLA Ops:
  0.6 0.0 copy-start.2
  0.6 0.0 copy-start.3
  0.7 0.0 copy-start.4
  0.7 0.7 %copy-done.2 = f32[512]{0:T(512)S(1)} copy-done((f32[512]{0:T(512)S(1)}, f32[512]{0:T(512)}, u32[]{:S(2)}) %copy-start.2) | copy-done | bytes 2072
  1.3 0.0 copy-done.3
  1.3 0.0 copy-done.4
  1.3 0.0 copy-start
  1.3 1.2 %copy-done = bf16[512,1024]{1,0:T(8,128)(2,1)S(1)} copy-done((bf16[512,1024]{1,0:T(8,128)(2,1)S(1)}, bf16[512,1024]{1,0:T(8,128)(2,1)}, u32[]{:S(2)}) %copy-start) | copy-done | bytes 1048600
  2.6 0.0 copy-start.1
  2.6 0.7 %copy-done.1 = s32[8,16]{1,0:T(8,128)S(1)} copy-done((s32[8,16]{1,0:T(8,128)S(1)}, s32[8,16]{1,0:T(8,128)}, u32[]{:S(2)}) %copy-start.1) | copy-done | bytes 536
  3.2 0.0 copy-start.5
  3.2 0.7 %copy-done.5 = s32[8]{0:T(128)S(1)} copy-done((s32[8]{0:T(128)S(1)}, s32[8]{0:T(128)}, u32[]{:S(2)}) %copy-start.5) | copy-done | bytes 56
  3.9 0.0 copy-start.6
  3.9 0.7 %copy-done.6 = s32[8]{0:T(128)S(1)} copy-done((s32[8]{0:T(128)S(1)}, s32[8]{0:T(128)}, u32[]{:S(2)}) %copy-start.6) | copy-done | bytes 56
  4.6 23.7 %square_collocate.1 = (bf16[512,256]{1,0:T(8,128)(2,1)S(1)}, f32[32,16,128]{2,1,0:T(8,128)S(1)}) custom-call(bf16[512,1024]{1,0:T(8,128)(2,1)S(1)} %copy-done, s32[8,16]{1,0:T(8,128)S(1)} %copy-done.1, f32[1,256]{1,0:T(1,128)S(1)} %bitcast.3, f32[1,512]{1,0:T(1,128)S(1)} %bitcast.2, s32[8]{0:T(128)S(1)} %copy-done.4, s32[8]{0:T(128)S(1)} %copy-done.5, ...), custom_call_target="tpu_custom_call" | custom-call | tf_op jit(solution)/shard_map/square_collocate/pallas_call | solution.py:317
  28.3 0.7 %copy.11 = bf16[512,256]{1,0:T(8,128)(2,1)} copy(bf16[512,256]{1,0:T(8,128)(2,1)S(1)} %get-tuple-element.4) | data formatting | bytes 524288
  29.0 0.7 %copy.12 = f32[32,16,128]{2,1,0:T(8,128)} copy(f32[32,16,128]{2,1,0:T(8,128)S(1)} %get-tuple-element.5) | data formatting | bytes 524288
Async XLA Ops:
  0.6 0.7 %copy-start.2 = (f32[512]{0:T(512)S(1)}, f32[512]{0:T(512)}, u32[]{:S(2)}) copy-start(f32[512]{0:T(512)} %param.10) | copy-start | bytes 6148
  0.6 0.7 %copy-start.3 = (f32[256]{0:T(256)S(1)}, f32[256]{0:T(256)}, u32[]{:S(2)}) copy-start(f32[256]{0:T(256)} %param.9) | copy-start | bytes 3076
  0.7 0.7 %copy-start.4 = (s32[8]{0:T(128)S(1)}, s32[8]{0:T(128)}, u32[]{:S(2)}) copy-start(s32[8]{0:T(128)} %ax_ref.1) | copy-start | bytes 100
  1.3 1.2 %copy-start = (bf16[512,1024]{1,0:T(8,128)(2,1)S(1)}, bf16[512,1024]{1,0:T(8,128)(2,1)}, u32[]{:S(2)}) copy-start(bf16[512,1024]{1,0:T(8,128)(2,1)} %a_ref.1) | copy-start | bytes 3145732
  2.6 0.7 %copy-start.1 = (s32[8,16]{1,0:T(8,128)S(1)}, s32[8,16]{1,0:T(8,128)}, u32[]{:S(2)}) copy-start(s32[8,16]{1,0:T(8,128)} %mask_ref.1) | copy-start | bytes 1540
  3.2 0.7 %copy-start.5 = (s32[8]{0:T(128)S(1)}, s32[8]{0:T(128)}, u32[]{:S(2)}) copy-start(s32[8]{0:T(128)} %ay_ref.1) | copy-start | bytes 100
  3.9 0.7 %copy-start.6 = (s32[8]{0:T(128)S(1)}, s32[8]{0:T(128)}, u32[]{:S(2)}) copy-start(s32[8]{0:T(128)} %az_ref.1) | copy-start | bytes 100

commit v2 on v1

v2 whole, which is shorter than its diff:
```python
import functools

import jax
import jax.numpy as jnp
from jax import lax
from jax.experimental import pallas as pl
from jax.experimental.pallas import tpu as pltpu
from jax.sharding import PartitionSpec as P

BLOCK = 64
TILE = 16
SX = 32
SY = 16
GZ = 128
STEP_SQ = 0.0625
MESH = pl.DeviceIdType.MESH
F32 = jnp.float32
BF16 = jnp.bfloat16
LANES = 128
OUT_CHUNKS = 2
LOADS = 2


def dot_nt(a, b):
    return lax.dot_general(a, b, (((1,), (1,)), ((), ())), preferred_element_type=F32)


def hi_lo(x):
    high = x.astype(BF16).astype(F32)
    return jnp.concatenate([high, x - high], axis=0).astype(BF16)


def kernel(
    sizes,
    a_hbm, mask_hbm, w_hbm, e_hbm, ax_hbm, ay_hbm, az_hbm,
    sq_ref, den_ref,
    a_ref, mask_ref, w_ref, e_ref, ax_ref, ay_ref, az_ref, load_sem,
    m_buf, right, part_out, part_in, w_all, v_out, v_all, q_out, q_all, pack, pack_in, shape_xy, shape_low, shape_z,
    piece_send, piece_recv, fwd_send, part_send, part_recv,
    w_send, w_recv, v_send, v_recv, q_send, q_recv, pack_send, pack_recv,
):
    nr, nc, nl = sizes
    ratio = nr // nc
    rows, cols = a_ref.shape
    width = cols // nl
    atoms = rows // BLOCK
    r, c, l = lax.axis_index("row"), lax.axis_index("col"), lax.axis_index("layer")
    sibling = r + 1 - 2 * (r % 2)
    following = (r + 1) % nr

    def remote(src, dst, send, recv, device):
        return pltpu.make_async_remote_copy(
            src_ref=src, dst_ref=dst, send_sem=send, recv_sem=recv,
            device_id=device, device_id_type=MESH,
        )

    chunks = width // LANES
    tall = rows // LOADS
    small = [
        pltpu.make_async_copy(src, dst, load_sem.at[at])
        for at, (src, dst) in enumerate((
            (mask_hbm, mask_ref), (w_hbm, w_ref), (e_hbm, e_ref),
            (ax_hbm, ax_ref), (ay_hbm, ay_ref), (az_hbm, az_ref),
        ))
    ]
    large = [
        pltpu.make_async_copy(
            a_hbm.at[pl.ds(p * tall, tall), :], a_ref.at[pl.ds(p * tall, tall), :], load_sem.at[6 + p]
        )
        for p in range(LOADS)
    ]
    for copy in small + large:
        copy.start()

    barrier = pltpu.get_barrier_semaphore()
    peers = 0
    for dr in range(nr):
        for dc in range(nc):
            if dr or dc:
                peers += 1
                pl.semaphore_signal(
                    barrier, inc=1, device_id=((r + dr) % nr, (c + dc) % nc, l), device_id_type=MESH
                )
    for k in range(1, nl):
        peers += 1
        pl.semaphore_signal(barrier, inc=1, device_id=(r, c, (l + k) % nl), device_id_type=MESH)

    for copy in small:
        copy.wait()
    kept = jnp.where(mask_ref[...] > 0, 1.0, 0.0).astype(F32)
    spread = lax.broadcasted_iota(jnp.int32, (cols // BLOCK, cols), 1) // BLOCK
    pick = lax.broadcasted_iota(jnp.int32, (cols // BLOCK, cols), 0)
    wide = jnp.dot(kept, jnp.where(spread == pick, 1.0, 0.0).astype(F32), preferred_element_type=F32)
    w_all[l] = jnp.broadcast_to(w_ref[...], (8, width))
    lane_atom = lax.broadcasted_iota(jnp.int32, (8, rows), 1) // BLOCK
    sub = lax.broadcasted_iota(jnp.int32, (8, rows), 0)
    table = jnp.broadcast_to(e_ref[...], (8, rows))
    for j in range(atoms):
        here = lane_atom == j
        for at, ref in ((1, ax_ref), (2, ay_ref), (3, az_ref)):
            table = jnp.where(here & (sub == at), ref[j].astype(F32), table)
    pack[...] = table
    for b in range(atoms):
        if b % (atoms // LOADS) == 0:
            large[b // (atoms // LOADS)].wait()
        at = pl.ds(b * BLOCK, BLOCK)
        m_buf[at, :] = a_ref[at, :] * jnp.broadcast_to(wide[b : b + 1, :], (BLOCK, cols)).astype(BF16)

    pl.semaphore_wait(barrier, peers)

    w_copies = [
        remote(w_all.at[l], w_all.at[l], w_send.at[k - 1], w_recv.at[k - 1], (r, c, (l + k) % nl))
        for k in range(1, nl)
    ]
    for copy in w_copies:
        copy.start()
    pack_copy = remote(pack, pack_in, pack_send.at[0], pack_recv.at[0], (following, c, l))
    pack_copy.start()

    home = r // ratio
    slot = r % ratio

    def strip(h):
        return m_buf.at[:, pl.ds(pl.multiple_of(l * width + h * LANES, LANES), LANES)]

    def piece(i, cc, h):
        return right.at[i, cc, h]

    def sem_at(i, cc, h):
        return (i * nc + cc) * chunks + h

    def piece_copy(k, h):
        return remote(
            strip(h), piece(slot, c, h), piece_send.at[k * chunks + h],
            piece_recv.at[sem_at(slot, c, h)], ((r + 2 * k) % nr, home, l),
        )

    def own_copy(h):
        return pltpu.make_async_copy(strip(h), piece(slot, c, h), piece_recv.at[sem_at(slot, c, h)])

    at_home = home == c
    for h in range(chunks):
        for k in range(1, nr // 2):
            piece_copy(k, h).start()

        @pl.when(at_home)
        def _():
            own_copy(h).start()

        @pl.when(jnp.logical_not(at_home))
        def _():
            piece_copy(0, h).start()

    y_first = (c * nl + l) * SY
    y_count = nc * nl * SY

    def profiles(g, ref):
        rate = ref[0:1, :] * (-STEP_SQ)

        def profile(t):
            value = jnp.exp(rate * (t - 7.5) * (t - 7.5))
            return jnp.where((t >= 0.0) & (t < float(TILE)), value, 0.0)

        tx = lax.broadcasted_iota(jnp.int32, (SX, rows), 0).astype(F32) + float(g * SX) - ref[1:2, :]
        ty = (lax.broadcasted_iota(jnp.int32, (SY, rows), 0) + y_first).astype(F32) - ref[2:3, :]
        ty = jnp.where(ty < 0.0, ty + float(y_count), ty)
        tz = lax.broadcasted_iota(jnp.int32, (GZ, rows), 0).astype(F32) - ref[3:4, :]
        tz = jnp.where(tz < 0.0, tz + float(GZ), tz)
        px, py = profile(tx), profile(ty)
        for x in range(SX):
            plane = px[x : x + 1, :] * py
            high = plane.astype(BF16)
            shape_xy[g, x * SY : (x + 1) * SY, :] = high
            shape_low[g, x * SY : (x + 1) * SY, :] = (plane - high.astype(F32)).astype(BF16)
        shape_z[g] = profile(tz)

    profiles(0, pack)

    for copy in w_copies:
        copy.wait_recv()
    total = jnp.zeros((16, rows), F32)
    for k in range(nl):
        total = total + dot_nt(hi_lo(w_all[k]), m_buf[:, k * width : (k + 1) * width])
    v_out[...] = total[:8] + total[8:]

    def v_copy(k):
        return remote(
            v_out, v_all.at[slot, c], v_send.at[k], v_recv.at[slot * nc + c], ((r + k) % nr, home, l)
        )

    @pl.when(at_home)
    def _():
        v_all[slot, c] = v_out[...]

    @pl.when(jnp.logical_not(at_home))
    def _():
        v_copy(0).start()

    for k in range(1, nr):
        v_copy(k).start()

    pack_copy.wait_recv()
    profiles(1, pack_in)

    def direct(i):
        return (c * ratio + i) % 2 == r % 2

    def fwd_copy(i, cc, h):
        return remote(
            piece(i, cc, h), piece(i, cc, h), fwd_send.at[sem_at(i, cc, h)],
            piece_recv.at[sem_at(i, cc, h)], (sibling, c, l),
        )

    def landed(i, cc, h):
        fwd_copy(i, cc, h).wait_recv()

    def pass_on(h):
        for k in range(nc):
            cc = (c + 1 + k) % nc
            for i in range(ratio):

                @pl.when(direct(i))
                def _():
                    mine = (c * ratio + i == r) & (cc == c)

                    @pl.when(mine)
                    def _():
                        own_copy(h).wait()

                    @pl.when(jnp.logical_not(mine))
                    def _():
                        landed(i, cc, h)

                    fwd_copy(i, cc, h).start()

    def take(cc, h):
        for i in range(ratio):

            @pl.when(jnp.logical_not(direct(i)))
            def _():
                landed(i, cc, h)

    low = rows // OUT_CHUNKS

    def product(cc, h, at):
        total = jnp.dot(m_buf[at, 0:rows], right[0, cc, h], preferred_element_type=F32)
        for i in range(1, ratio):
            total = total + jnp.dot(
                m_buf[at, i * rows : (i + 1) * rows], right[i, cc, h], preferred_element_type=F32
            )
        return total

    def part_copy(k, h, o):
        at = pl.ds(o * low, low)
        index = ((k - 1) * chunks + h) * OUT_CHUNKS + o
        return remote(
            part_out.at[k - 1, h, at, :], part_in.at[k - 1, h, at, :], part_send.at[index],
            part_recv.at[index], (r, (c + k) % nc, l),
        )

    def parts(h):
        for k in range(1, nc):
            take((c + k) % nc, h)
            for o in range(OUT_CHUNKS):
                at = pl.ds(o * low, low)
                part_out[k - 1, h, at, :] = product((c + k) % nc, h, at).astype(BF16)
                part_copy(k, h, o).start()

    def charge_share():
        for i in range(ratio):
            for cc in range(nc):

                @pl.when(jnp.logical_not((c * ratio + i == r) & (cc == c)))
                def _():
                    remote(
                        v_out, v_all.at[i, cc], v_send.at[0], v_recv.at[i * nc + cc], (r, c, l)
                    ).wait_recv()

        total = jnp.zeros((16, rows), F32)
        for i in range(ratio):
            v = v_all[i, 0]
            for cc in range(1, nc):
                v = v + v_all[i, cc]
            total = total + dot_nt(hi_lo(v), m_buf[:, i * rows : (i + 1) * rows])
        q_out[...] = total[:8] + total[8:]
        q_all[0, c] = q_out[...]

    def q_copy(g, k):
        return remote(
            q_out, q_all.at[g, c], q_send.at[g * nc + k], q_recv.at[g * nc + k],
            ((r + g) % nr, (c + k) % nc, l),
        )

    sent_q = [(g, k) for g in range(2) for k in range(nc) if g or k]
    for h in range(chunks):
        pass_on(h)
        if h == chunks - 1:
            charge_share()
            for g, k in sent_q:
                q_copy(g, k).start()
        parts(h)

    for g, k in sent_q:
        q_copy(g, k).wait_recv()
    total = jnp.zeros((SX * SY, GZ), F32)
    for g in range(2):
        charge = q_all[g, 0]
        for cc in range(1, nc):
            charge = charge + q_all[g, cc]
        value = shape_z[g] * charge[0:1, :]
        high = value.astype(BF16)
        rest = (value - high.astype(F32)).astype(BF16)
        total = total + dot_nt(shape_xy[g], high) + dot_nt(shape_xy[g], rest) + dot_nt(shape_low[g], high)
    den_ref[...] = total.reshape(SX, SY, GZ)

    for h in range(chunks):
        take(c, h)
        for o in range(OUT_CHUNKS):
            at = pl.ds(o * low, low)
            total = product(c, h, at)
            for k in range(1, nc):
                part_copy(k, h, o).wait_recv()
                total = total + part_in[k - 1, h, at, :].astype(F32)
            sq_ref[at, h * LANES : (h + 1) * LANES] = total.astype(BF16)

    for copy in w_copies:
        copy.wait_send()
    pack_copy.wait_send()
    for k in range(1, nr):
        v_copy(k).wait_send()
    for g, k in sent_q:
        q_copy(g, k).wait_send()
    for h in range(chunks):
        for k in range(1, nr // 2):
            piece_copy(k, h).wait_send()
        for i in range(ratio):
            for cc in range(nc):

                @pl.when(direct(i))
                def _():
                    fwd_copy(i, cc, h).wait_send()

    @pl.when(jnp.logical_not(at_home))
    def _():
        v_copy(0).wait_send()
        for h in range(chunks):
            piece_copy(0, h).wait_send()

    for k in range(1, nc):
        for h in range(chunks):
            for o in range(OUT_CHUNKS):
                part_copy(k, h, o).wait_send()


def local(sizes, density_matrix, block_mask, weights, exponents, anchor_x, anchor_y, anchor_z):
    nr, nc, nl = sizes
    ratio = nr // nc
    rows, cols = density_matrix.shape
    width = cols // nl
    dma = pltpu.SemaphoreType.DMA
    chunks = width // LANES
    pieces = ratio * nc * chunks
    outs = (nc - 1) * chunks * OUT_CHUNKS
    hbm = pl.BlockSpec(memory_space=pltpu.HBM)
    vmem = pl.BlockSpec(memory_space=pltpu.VMEM)
    return pl.pallas_call(
        functools.partial(kernel, sizes),
        out_shape=(
            jax.ShapeDtypeStruct((rows, width), BF16),
            jax.ShapeDtypeStruct((SX, SY, GZ), F32),
        ),
        in_specs=[hbm] * 7,
        out_specs=(vmem, vmem),
        scratch_shapes=[
            pltpu.VMEM((rows, cols), BF16),
            pltpu.VMEM(block_mask.shape, jnp.int32),
            pltpu.VMEM((1, width), F32),
            pltpu.VMEM((1, rows), F32),
            pltpu.SMEM(anchor_x.shape, jnp.int32),
            pltpu.SMEM(anchor_x.shape, jnp.int32),
            pltpu.SMEM(anchor_x.shape, jnp.int32),
            dma((6 + LOADS,)),
            pltpu.VMEM((rows, cols), BF16),
            pltpu.VMEM((ratio, nc, chunks, rows, LANES), BF16),
            pltpu.VMEM((nc - 1, chunks, rows, LANES), BF16),
            pltpu.VMEM((nc - 1, chunks, rows, LANES), BF16),
            pltpu.VMEM((nl, 8, width), F32),
            pltpu.VMEM((8, rows), F32),
            pltpu.VMEM((ratio, nc, 8, rows), F32),
            pltpu.VMEM((8, rows), F32),
            pltpu.VMEM((2, nc, 8, rows), F32),
            pltpu.VMEM((8, rows), F32),
            pltpu.VMEM((8, rows), F32),
            pltpu.VMEM((2, SX * SY, rows), BF16),
            pltpu.VMEM((2, SX * SY, rows), BF16),
            pltpu.VMEM((2, GZ, rows), F32),
            dma((nr // 2 * chunks,)),
            dma((pieces,)),
            dma((pieces,)),
            dma((outs,)),
            dma((outs,)),
            dma((nl - 1,)),
            dma((nl - 1,)),
            dma((nr,)),
            dma((ratio * nc,)),
            dma((2 * nc,)),
            dma((2 * nc,)),
            dma((1,)),
            dma((1,)),
        ],
        compiler_params=pltpu.CompilerParams(
            collective_id=0, has_side_effects=True, vmem_limit_bytes=67_043_328
        ),
        name="square_collocate",
    )(
        density_matrix, block_mask, weights.reshape(1, -1), exponents.reshape(1, -1),
        anchor_x, anchor_y, anchor_z,
    )


def solution(mesh):
    sizes = (mesh.shape["row"], mesh.shape["col"], mesh.shape["layer"])
    return jax.shard_map(
        functools.partial(local, sizes),
        mesh=mesh,
        in_specs=(
            P("row", "col"), P("row", "col"), P(("col", "layer")),
            P("row"), P("row"), P("row"), P("row"),
        ),
        out_specs=(P("row", ("col", "layer")), P("row", ("col", "layer"), None)),
        check_vma=False,
    )
```

time: 29.9 us -> 25.6 us (0.86)
  the two profiles are of different devices: /device:TPU:0 before, /device:TPU:1 now
where the time goes in v2:
time: 25.6 us; the launch traced here: 25.5 us
  Pallas kernels  22.4 us (88%)
  local copies, waits for them, and re-layouts  2.42 us (9%)
  between operations  0.65 us (3%)
    pallas_call x1, Pallas kernels, local(): pl.pallas_call(functools.partial(kernel, sizes), out_shape=(jax.ShapeDtyp...  22.4 us
    unnamed x4, local copies, waits for them, and re-layouts  2.42 us

profile of v2, /device:TPU:1, one launch (start us, length us, event | category | flops | bytes accessed | tf_op | source)
XLA Modules:
  0.0 25.5 jit_solution(8185321999111237674)
XLA Ops:
  0.6 22.4 %square_collocate.1 = (bf16[512,256]{1,0:T(8,128)(2,1)}, f32[32,16,128]{2,1,0:T(8,128)}) custom-call(bf16[512,1024]{1,0:T(8,128)(2,1)} %a_hbm.1, s32[8,16]{1,0:T(8,128)} %mask_hbm.1, f32[1,256]{1,0:T(1,128)} %bitcast.3, f32[1,512]{1,0:T(1,128)} %bitcast.2, s32[8]{0:T(128)} %ax_hbm.1, s32[8]{0:T(128)} %ay_hbm.1, s32[8]{0:T(128)} %az_hbm.1), custom_call_target="tpu_custom_call" | custom-call | tf_op jit(solution)/shard_map/square_collocate/pallas_call | solution.py:366
  23.0 0.0 copy-start
  23.0 1.7 %copy.11 = bf16[512,256]{1,0:T(8,128)(2,1)} copy(bf16[512,256]{1,0:T(8,128)(2,1)} %get-tuple-element.4) | data formatting | bytes 524288
  24.8 0.0 copy-done
  24.8 0.7 %copy.12 = f32[32,16,128]{2,1,0:T(8,128)} copy(f32[32,16,128]{2,1,0:T(8,128)S(1)} %copy-done) | data formatting | bytes 524288
Async XLA Ops:
  23.0 1.7 %copy-start = (f32[32,16,128]{2,1,0:T(8,128)S(1)}, f32[32,16,128]{2,1,0:T(8,128)}, u32[]{:S(2)}) copy-start(f32[32,16,128]{2,1,0:T(8,128)} %get-tuple-element.5) | copy-start | bytes 786436

commit v3 on v2

--- a/solution.py
+++ b/solution.py
@@ -352,6 +352,17 @@
                 part_copy(k, h, o).wait_send()
 
 
+def store(sq_ref, den_ref, sq_out, den_out, sem):
+    copies = [
+        pltpu.make_async_copy(sq_ref, sq_out, sem.at[0]),
+        pltpu.make_async_copy(den_ref, den_out, sem.at[1]),
+    ]
+    for copy in copies:
+        copy.start()
+    for copy in copies:
+        copy.wait()
+
+
 def local(sizes, density_matrix, block_mask, weights, exponents, anchor_x, anchor_y, anchor_z):
     nr, nc, nl = sizes
     ratio = nr // nc
@@ -363,12 +374,17 @@
     outs = (nc - 1) * chunks * OUT_CHUNKS
     hbm = pl.BlockSpec(memory_space=pltpu.HBM)
     vmem = pl.BlockSpec(memory_space=pltpu.VMEM)
-    return pl.pallas_call(
+    inputs = (
+        density_matrix, block_mask, weights.reshape(1, -1), exponents.reshape(1, -1),
+        anchor_x, anchor_y, anchor_z,
+    )
+    shapes = (
+        jax.ShapeDtypeStruct((rows, width), BF16),
+        jax.ShapeDtypeStruct((SX, SY, GZ), F32),
+    )
+    results = pl.pallas_call(
         functools.partial(kernel, sizes),
-        out_shape=(
-            jax.ShapeDtypeStruct((rows, width), BF16),
-            jax.ShapeDtypeStruct((SX, SY, GZ), F32),
-        ),
+        out_shape=(pltpu.VMEM((rows, width), BF16), pltpu.VMEM((SX, SY, GZ), F32)),
         in_specs=[hbm] * 7,
         out_specs=(vmem, vmem),
         scratch_shapes=[
@@ -409,13 +425,19 @@
             dma((1,)),
         ],
         compiler_params=pltpu.CompilerParams(
-            collective_id=0, has_side_effects=True, vmem_limit_bytes=67_043_328
+            collective_id=0, has_side_effects=True, vmem_limit_bytes=66_000_000
         ),
         name="square_collocate",
-    )(
-        density_matrix, block_mask, weights.reshape(1, -1), exponents.reshape(1, -1),
-        anchor_x, anchor_y, anchor_z,
-    )
+    )(*[pltpu.with_memory_space_constraint(x, pltpu.HBM) for x in inputs])
+    return pl.pallas_call(
+        store,
+        out_shape=shapes,
+        in_specs=[vmem] * 2,
+        out_specs=(hbm, hbm),
+        scratch_shapes=[dma((2,))],
+        compiler_params=pltpu.CompilerParams(vmem_limit_bytes=4 * 1024 * 1024),
+        name="store",
+    )(*results)
 
 
 def solution(mesh):

time: 25.6 us -> 23.3 us (0.910)
  local copies, waits for them, and re-layouts: 2.42 us -> 0 us
    unnamed x4 -> x0, local copies, waits for them, and re-layouts: 2.42 us -> none
    pallas_call x1 -> x2, Pallas kernels: 22.4 us -> 22.4 us  [the longest x1 21.6 us: local(): pl.pallas_call(functools.partial(kernel, sizes), out_shape=(pltpu.VMEM((r...]
where the time goes in v3:
time: 23.3 us; the launch traced here: 23.1 us
  Pallas kernels  22.4 us (96%)
  between operations  0.64 us (3%)
    pallas_call x1, Pallas kernels, local(): pl.pallas_call(functools.partial(kernel, sizes), out_shape=(pltpu.VMEM((r...  21.6 us
    pallas_call x1, Pallas kernels, local(): pl.pallas_call(store, out_shape=shapes, in_specs=[vmem] * 2, out_specs=(h...  0.81 us

profile of v3, /device:TPU:1, one launch (start us, length us, event | category | flops | bytes accessed | tf_op | source)
XLA Modules:
  0.0 23.1 jit_solution(6650268185179460855)
XLA Ops:
  0.6 21.6 %square_collocate.1 = (bf16[512,256]{1,0:T(8,128)(2,1)S(1)}, f32[32,16,128]{2,1,0:T(8,128)S(1)}) custom-call(bf16[512,1024]{1,0:T(8,128)(2,1)} %a_hbm.1, s32[8,16]{1,0:T(8,128)} %mask_hbm.1, f32[1,256]{1,0:T(1,128)} %bitcast.3, f32[1,512]{1,0:T(1,128)} %bitcast.2, s32[8]{0:T(128)} %ax_hbm.1, s32[8]{0:T(128)} %ay_hbm.1, s32[8]{0:T(128)} %az_hbm.1), custom_call_target="tpu_custom_call" | custom-call | tf_op jit(solution)/shard_map/square_collocate/pallas_call | solution.py:385
  22.3 0.8 %store.1 = (bf16[512,256]{1,0:T(8,128)(2,1)}, f32[32,16,128]{2,1,0:T(8,128)}) custom-call(bf16[512,256]{1,0:T(8,128)(2,1)S(1)} %get-tuple-element.4.sq_ref, f32[32,16,128]{2,1,0:T(8,128)S(1)} %get-tuple-element.5.den_ref), custom_call_target="tpu_custom_call" | custom-call | tf_op jit(solution)/shard_map/store/pallas_call | solution.py:432

commit v4 on v3

--- a/solution.py
+++ b/solution.py
@@ -35,7 +35,7 @@
     a_hbm, mask_hbm, w_hbm, e_hbm, ax_hbm, ay_hbm, az_hbm,
     sq_ref, den_ref,
     a_ref, mask_ref, w_ref, e_ref, ax_ref, ay_ref, az_ref, load_sem,
-    m_buf, right, part_out, part_in, w_all, v_out, v_all, q_out, q_all, pack, pack_in, shape_xy, shape_low, shape_z,
+    m_buf, right, own_part, part_out, part_in, w_all, v_out, v_all, q_out, q_all, pack, pack_in, shape_xy, shape_low, shape_z,
     piece_send, piece_recv, fwd_send, part_send, part_recv,
     w_send, w_recv, v_send, v_recv, q_send, q_recv, pack_send, pack_recv,
 ):
@@ -300,6 +300,12 @@
                 q_copy(g, k).start()
         parts(h)
 
+    for h in range(chunks):
+        take(c, h)
+        for o in range(OUT_CHUNKS):
+            at = pl.ds(o * low, low)
+            own_part[h, at, :] = product(c, h, at)
+
     for g, k in sent_q:
         q_copy(g, k).wait_recv()
     total = jnp.zeros((SX * SY, GZ), F32)
@@ -314,10 +320,9 @@
     den_ref[...] = total.reshape(SX, SY, GZ)
 
     for h in range(chunks):
-        take(c, h)
         for o in range(OUT_CHUNKS):
             at = pl.ds(o * low, low)
-            total = product(c, h, at)
+            total = own_part[h, at, :]
             for k in range(1, nc):
                 part_copy(k, h, o).wait_recv()
                 total = total + part_in[k - 1, h, at, :].astype(F32)
@@ -398,6 +403,7 @@
             dma((6 + LOADS,)),
             pltpu.VMEM((rows, cols), BF16),
             pltpu.VMEM((ratio, nc, chunks, rows, LANES), BF16),
+            pltpu.VMEM((chunks, rows, LANES), F32),
             pltpu.VMEM((nc - 1, chunks, rows, LANES), BF16),
             pltpu.VMEM((nc - 1, chunks, rows, LANES), BF16),
             pltpu.VMEM((nl, 8, width), F32),

time: 23.3 us -> 22.6 us (0.970)
  the two profiles are of different devices: /device:TPU:1 before, /device:TPU:0 now
where the time goes in v4:
time: 22.6 us; the launch traced here: 22.4 us
  Pallas kernels  21.8 us (96%)
  between operations  0.64 us (3%)
    pallas_call x1, Pallas kernels, local(): pl.pallas_call(functools.partial(kernel, sizes), out_shape=(pltpu.VMEM((r...  21 us
    pallas_call x1, Pallas kernels, local(): pl.pallas_call(store, out_shape=shapes, in_specs=[vmem] * 2, out_specs=(h...  0.81 us

profile of v4, /device:TPU:0, one launch (start us, length us, event | category | flops | bytes accessed | tf_op | source)
XLA Modules:
  0.0 22.4 jit_solution(1423581517980012625)
XLA Ops:
  0.6 21.0 %square_collocate.1 = (bf16[512,256]{1,0:T(8,128)(2,1)S(1)}, f32[32,16,128]{2,1,0:T(8,128)S(1)}) custom-call(bf16[512,1024]{1,0:T(8,128)(2,1)} %a_hbm.1, s32[8,16]{1,0:T(8,128)} %mask_hbm.1, f32[1,256]{1,0:T(1,128)} %bitcast.3, f32[1,512]{1,0:T(1,128)} %bitcast.2, s32[8]{0:T(128)} %ax_hbm.1, s32[8]{0:T(128)} %ay_hbm.1, s32[8]{0:T(128)} %az_hbm.1), custom_call_target="tpu_custom_call" | custom-call | tf_op jit(solution)/shard_map/square_collocate/pallas_call | solution.py:390
  21.6 0.8 %store.1 = (bf16[512,256]{1,0:T(8,128)(2,1)}, f32[32,16,128]{2,1,0:T(8,128)}) custom-call(bf16[512,256]{1,0:T(8,128)(2,1)S(1)} %get-tuple-element.4.sq_ref, f32[32,16,128]{2,1,0:T(8,128)S(1)} %get-tuple-element.5.den_ref), custom_call_target="tpu_custom_call" | custom-call | tf_op jit(solution)/shard_map/store/pallas_call | solution.py:438

commit v5 on v4

--- a/solution.py
+++ b/solution.py
@@ -139,7 +139,7 @@
         return pltpu.make_async_copy(strip(h), piece(slot, c, h), piece_recv.at[sem_at(slot, c, h)])
 
     at_home = home == c
-    for h in range(chunks):
+    def start_strips(h):
         for k in range(1, nr // 2):
             piece_copy(k, h).start()
 
@@ -150,6 +150,8 @@
         @pl.when(jnp.logical_not(at_home))
         def _():
             piece_copy(0, h).start()
+
+    start_strips(0)
 
     y_first = (c * nl + l) * SY
     y_count = nc * nl * SY
@@ -198,6 +200,8 @@
 
     for k in range(1, nr):
         v_copy(k).start()
+    for h in range(1, chunks):
+        start_strips(h)
 
     pack_copy.wait_recv()
     profiles(1, pack_in)
@@ -294,7 +298,7 @@
     sent_q = [(g, k) for g in range(2) for k in range(nc) if g or k]
     for h in range(chunks):
         pass_on(h)
-        if h == chunks - 1:
+        if h == 0:
             charge_share()
             for g, k in sent_q:
                 q_copy(g, k).start()

time: 22.6 us -> 23.5 us (1.040)
  Pallas kernels: 21.8 us -> 22.6 us
    pallas_call x1, Pallas kernels: 21 us -> 21.8 us  [local(): pl.pallas_call(functools.partial(kernel, sizes), out_shape=(pltpu.VMEM((r...]
where the time goes in v5:
time: 23.5 us; the launch traced here: 23.3 us
  Pallas kernels  22.6 us (96%)
  between operations  0.64 us (3%)
    pallas_call x1, Pallas kernels, local(): pl.pallas_call(functools.partial(kernel, sizes), out_shape=(pltpu.VMEM((r...  21.8 us
    pallas_call x1, Pallas kernels, local(): pl.pallas_call(store, out_shape=shapes, in_specs=[vmem] * 2, out_specs=(h...  0.81 us

profile of v5, /device:TPU:0, one launch (start us, length us, event | category | flops | bytes accessed | tf_op | source)
XLA Modules:
  0.0 23.3 jit_solution(15104618231128296234)
XLA Ops:
  0.6 21.8 %square_collocate.1 = (bf16[512,256]{1,0:T(8,128)(2,1)S(1)}, f32[32,16,128]{2,1,0:T(8,128)S(1)}) custom-call(bf16[512,1024]{1,0:T(8,128)(2,1)} %a_hbm.1, s32[8,16]{1,0:T(8,128)} %mask_hbm.1, f32[1,256]{1,0:T(1,128)} %bitcast.3, f32[1,512]{1,0:T(1,128)} %bitcast.2, s32[8]{0:T(128)} %ax_hbm.1, s32[8]{0:T(128)} %ay_hbm.1, s32[8]{0:T(128)} %az_hbm.1), custom_call_target="tpu_custom_call" | custom-call | tf_op jit(solution)/shard_map/square_collocate/pallas_call | solution.py:394
  22.5 0.8 %store.1 = (bf16[512,256]{1,0:T(8,128)(2,1)}, f32[32,16,128]{2,1,0:T(8,128)}) custom-call(bf16[512,256]{1,0:T(8,128)(2,1)S(1)} %get-tuple-element.4.sq_ref, f32[32,16,128]{2,1,0:T(8,128)S(1)} %get-tuple-element.5.den_ref), custom_call_target="tpu_custom_call" | custom-call | tf_op jit(solution)/shard_map/store/pallas_call | solution.py:442
